TPU v7x, 128 devices: a whole 4x4x4 slice. The times are simulated.
128 devices in a mesh: img: 4 (over z_lo, core), exp: 32 (over x, y, z_hi).
Axes of the slice: x: 4, y: 4, z: 4 (z_hi: 2, z_lo: 2; z = z_hi * 2 + z_lo), core: 2. Of those that a mesh axis runs over, the one named last changes fastest.
Arguments:
- context: bfloat16 [256, 256, 1024], P(('img', 'exp')), may hold values from -1.5 to 1.5
- residual: bfloat16 [256, 256, 1024], P(('img', 'exp')), may hold values from -1.5 to 1.5
- cotangent: bfloat16 [256, 256, 1024], P(('img', 'exp')), may hold values from -6 to 6
- proj_weight: bfloat16 [1024, 1024], P('img'), may hold values from -0.1875 to 0.1875
- slot_params: bfloat16 [1024, 64], replicated, may hold values from -0.1875 to 0.1875
- expert_in: bfloat16 [64, 1024, 4096], P('exp', None, 'img'), may hold values from -0.1875 to 0.1875
- expert_out: bfloat16 [64, 4096, 1024], P('exp', 'img'), may hold values from -0.09375 to 0.09375
Outputs:
- grad_context: bfloat16 [256, 256, 1024], P(('img', 'exp'))
- grad_residual: bfloat16 [256, 256, 1024], P(('img', 'exp'))
- grad_proj: float32 [1024, 1024], P('img')
- grad_slots: float32 [1024, 64], replicated
- grad_expert_in: bfloat16 [64, 1024, 4096], P('exp', None, 'img')
- grad_expert_out: bfloat16 [64, 4096, 1024], P('exp', 'img')
All inputs are finite; a program needn't handle non-finite values.
Results may differ from a plain program's by a relative error of at most 0.025.
Values may be sent and summed in bfloat16 or wider, within the bound.
A program may use at most 128 MiB of HBM per device.

v0:
```python
import math
import jax
import jax.numpy as jnp
from jax import lax
from jax.sharding import Mesh
from jax.sharding import PartitionSpec as P

IMG = ("img_0", "img_1")
IMG_EXP = ("img_0", "img_1", "exp")
logit_scale = 48.0
epsilon = 1e-06


def copy_for_each(shard, axis):
    devices = lax.axis_size(axis)
    return lax.all_to_all(
        jnp.broadcast_to(shard[None], (devices, *shard.shape)), axis, 0, 0, tiled=True
    )


def laid_out(pieces, dim):
    pieces = jnp.moveaxis(pieces, 0, dim)
    dims = pieces.shape
    return pieces.reshape(*dims[:dim], dims[dim] * dims[dim + 1], *dims[dim + 2 :])


def gather_directly(shard, axis, dim):
    pieces = copy_for_each(shard, axis)
    return laid_out(pieces, dim)


def split_up(shard, dim, devices):
    before, after = (shard.shape[:dim], shard.shape[dim + 1 :])
    return jnp.moveaxis(shard.reshape(*before, devices, -1, *after), dim, 0)


def summed_on_arrival(shard, axis, dim):
    devices = lax.axis_size(axis)
    pieces = lax.all_to_all(split_up(shard, dim, devices), axis, 0, 0, tiled=True)
    return jnp.sum(pieces.astype(jnp.float32), axis=0)


def sum_in_two_steps(shard, axes, dim):
    far, near = axes
    own = summed_on_arrival(split_up(shard, dim, lax.axis_size(far)), near, dim + 1)
    return jnp.sum(
        lax.all_to_all(own.astype(jnp.bfloat16), far, 0, 0, tiled=True).astype(jnp.float32), axis=0
    )


def padded_to(lines, devices):
    spare = -lines.shape[0] % devices
    if not spare:
        return lines
    return jnp.concatenate([lines, jnp.zeros((spare, *lines.shape[1:]), lines.dtype)])


def nested_sum(shard, axes):
    lines = shard.reshape(-1, shard.shape[-1])
    own = summed_on_arrival(padded_to(lines, lax.axis_size(axes)), axes, 0)
    whole = gather_directly(own.astype(jnp.bfloat16), axes, 0)
    return whole[: len(lines)].reshape(shard.shape).astype(jnp.float32)


def gelu_back(pre, upstream):
    return jax.vjp(jax.nn.gelu, pre)[1](upstream)[0]


def shards(context, residual, cotangent, proj_weight, slot_params, expert_in, expert_out):
    images, tokens, width = context.shape
    rows = images * tokens
    factor = logit_scale / math.sqrt(width)
    flat_ctx = context.reshape(rows, width)
    columns = flat_ctx
    mixed = jnp.dot(
        columns, gather_directly(proj_weight, IMG, 0), preferred_element_type=jnp.float32
    )
    stream = (residual.reshape(rows, width).astype(jnp.float32) + mixed).astype(jnp.bfloat16)
    stream32 = stream.astype(jnp.float32)
    inverse = lax.rsqrt(jnp.mean(stream32 * stream32, axis=-1, keepdims=True) + epsilon)
    normed32 = stream32 * inverse
    normed = normed32.astype(jnp.bfloat16)
    params32 = slot_params.astype(jnp.float32)
    slot_norm = jnp.sqrt(jnp.sum(params32 * params32, axis=0, keepdims=True) + epsilon)
    unit32 = params32 / slot_norm
    unit = unit32.astype(jnp.bfloat16)
    logits = factor * jnp.dot(normed, unit, preferred_element_type=jnp.float32)
    logits = logits.reshape(images, tokens, -1)
    expo = jnp.exp(logits)
    dispatch32 = expo / jnp.sum(expo, axis=1, keepdims=True)
    combine32 = expo / jnp.sum(expo, axis=2, keepdims=True)
    dispatch = dispatch32.astype(jnp.bfloat16)
    combine = combine32.astype(jnp.bfloat16)
    normed3 = normed.reshape(images, tokens, width)
    slot_in = jnp.einsum(
        "bms,bmd->bsd", dispatch, normed3, preferred_element_type=jnp.float32
    ).astype(jnp.bfloat16)
    sent = lax.all_to_all(slot_in, "exp", split_axis=1, concat_axis=0, tiled=True)
    slot_rows = gather_directly(sent, IMG, 0)
    pre = jnp.einsum("gjd,jdf->gjf", slot_rows, expert_in, preferred_element_type=jnp.float32)
    act = jax.nn.gelu(pre).astype(jnp.bfloat16)
    piece = act
    summed = summed_on_arrival(
        jnp.einsum("gjf,jfd->gjd", piece, expert_out, preferred_element_type=jnp.float32).astype(
            jnp.bfloat16
        ),
        IMG,
        0,
    )
    slot_out = lax.all_to_all(
        summed.astype(jnp.bfloat16), "exp", split_axis=0, concat_axis=1, tiled=True
    )
    grad_slot_out = jnp.einsum(
        "bms,bmd->bsd", combine, cotangent, preferred_element_type=jnp.float32
    ).astype(jnp.bfloat16)
    grad_sent = lax.all_to_all(grad_slot_out, "exp", split_axis=1, concat_axis=0, tiled=True)
    grad_gathered = gather_directly(grad_sent, IMG, 0)
    grad_combine = jnp.einsum(
        "bmd,bsd->bms", cotangent, slot_out, preferred_element_type=jnp.float32
    )
    grad_act = jnp.einsum(
        "gjd,jfd->gjf", grad_gathered, expert_out, preferred_element_type=jnp.float32
    )
    grad_pre = gelu_back(pre, grad_act).astype(jnp.bfloat16)
    grad_expert_out = jnp.einsum(
        "gjf,gjd->jfd", act, grad_gathered, preferred_element_type=jnp.float32
    ).astype(jnp.bfloat16)
    grad_expert_in = jnp.einsum(
        "gjd,gjf->jdf", slot_rows, grad_pre, preferred_element_type=jnp.float32
    ).astype(jnp.bfloat16)
    piece = grad_pre
    grad_summed = summed_on_arrival(
        jnp.einsum("gjf,jdf->gjd", piece, expert_in, preferred_element_type=jnp.float32).astype(
            jnp.bfloat16
        ),
        IMG,
        0,
    )
    grad_slot_in = lax.all_to_all(
        grad_summed.astype(jnp.bfloat16), "exp", split_axis=0, concat_axis=1, tiled=True
    )
    grad_dispatch = jnp.einsum(
        "bmd,bsd->bms", normed3, grad_slot_in, preferred_element_type=jnp.float32
    )
    grad_logits32 = combine32 * (
        grad_combine - jnp.sum(combine32 * grad_combine, axis=2, keepdims=True)
    )
    grad_logits32 = grad_logits32 + dispatch32 * (
        grad_dispatch - jnp.sum(dispatch32 * grad_dispatch, axis=1, keepdims=True)
    )
    grad_logits = grad_logits32.astype(jnp.bfloat16).reshape(rows, -1)
    grad_normed = jnp.einsum(
        "bms,bsd->bmd", dispatch, grad_slot_in, preferred_element_type=jnp.float32
    ).reshape(rows, width)
    grad_normed = grad_normed + factor * jnp.dot(
        grad_logits, unit.T, preferred_element_type=jnp.float32
    )
    local_unit = factor * jnp.dot(normed.T, grad_logits, preferred_element_type=jnp.float32)
    grad_unit = lax.psum(local_unit, IMG_EXP)
    grad_slots = (
        grad_unit - unit32 * jnp.sum(unit32 * grad_unit, axis=0, keepdims=True)
    ) / slot_norm
    upstream = cotangent.reshape(rows, width).astype(jnp.float32)
    grad_stream = upstream + inverse * (
        grad_normed - normed32 * jnp.mean(normed32 * grad_normed, axis=-1, keepdims=True)
    )
    grad_residual = grad_stream.astype(jnp.bfloat16)
    grad_context = jnp.dot(
        grad_residual, gather_directly(proj_weight, IMG, 0).T, preferred_element_type=jnp.float32
    ).astype(jnp.bfloat16)
    columns = flat_ctx
    owned = sum_in_two_steps(
        jnp.dot(columns.T, grad_residual, preferred_element_type=jnp.float32).astype(jnp.bfloat16),
        ("img_0", "img_1"),
        0,
    )
    grad_proj = nested_sum(owned.astype(jnp.bfloat16), "exp")
    return (
        grad_context.reshape(images, tokens, width),
        grad_residual.reshape(images, tokens, width),
        grad_proj,
        grad_slots,
        grad_expert_in,
        grad_expert_out,
    )


def solution(mesh):
    torus = Mesh(mesh.devices.reshape(2, 2, mesh.shape["exp"]), ("img_0", "img_1", "exp"))
    placed = (
        P(IMG_EXP, None, None),
        P(IMG_EXP, None, None),
        P(IMG_EXP, None, None),
        P(IMG, None),
        P(),
        P("exp", None, IMG),
        P("exp", IMG, None),
    )
    return jax.shard_map(
        shards,
        mesh=torus,
        in_specs=placed,
        out_specs=(
            P(IMG_EXP, None, None),
            P(IMG_EXP, None, None),
            P(IMG, None),
            P(),
            P("exp", None, IMG),
            P("exp", IMG, None),
        ),
        check_vma=False,
    )
```

profile of v0, /device:TPU:1, one launch (start us, length us, event | category | flops | bytes accessed | tf_op | source)
XLA Modules:
  0.0 417.2 jit_solution(16925801770048762867)
XLA Ops:
  7.2 2.7 broadcast_in_dim.12
  9.9 5.1 %all-to-all-start = ((bf16[4,256,1024]{2,1,0:T(8,128)(2,1)}), bf16[4,256,1024]{2,1,0:T(8,128)(2,1)S(1)}, u32[]{:S(2)}, u32[]{:S(2)}) async-start(bf16[4,256,1024]{2,1,0:T(8,128)(2,1)} %broadcast_in_dim.12), calls=%async_computation | async-start | bytes 4194304 | tf_op jit(solution)/shard_map/all_to_all | solution.py:16
  15.1 24.5 %all-to-all-done = bf16[4,256,1024]{2,1,0:T(8,128)(2,1)S(1)} async-done(((bf16[4,256,1024]{2,1,0:T(8,128)(2,1)}), bf16[4,256,1024]{2,1,0:T(8,128)(2,1)S(1)}, u32[]{:S(2)}, u32[]{:S(2)}) %all-to-all-start) | async-done | bytes 2097184 | tf_op jit(solution)/shard_map/all_to_all | solution.py:16
  39.7 1.3 copy-done.7
  41.0 3.2 fusion.10
  48.0 10.6 %all-to-all-start.3 = ((bf16[2,64,1024]{2,0,1:T(2,128)(2,1)}), bf16[2,64,1024]{2,0,1:T(2,128)(2,1)}, u32[]{:S(2)}, u32[]{:S(2)}) async-start(bf16[2,64,1024]{2,0,1:T(2,128)(2,1)} %copy.81), calls=%async_computation.3 | async-start | bytes 524288 | tf_op jit(solution)/shard_map/all_to_all | solution.py:98
  58.7 1.5 convolution_convert_fusion.7
  61.2 7.1 %all-to-all-done.3 = bf16[2,64,1024]{2,0,1:T(2,128)(2,1)} async-done(((bf16[2,64,1024]{2,0,1:T(2,128)(2,1)}), bf16[2,64,1024]{2,0,1:T(2,128)(2,1)}, u32[]{:S(2)}, u32[]{:S(2)}) %all-to-all-start.3) | async-done | bytes 262176 | tf_op jit(solution)/shard_map/all_to_all | solution.py:98
  68.2 4.6 %all-to-all-start.1 = ((bf16[2,64,1024]{2,0,1:T(2,128)(2,1)}), bf16[2,64,1024]{2,0,1:T(2,128)(2,1)}, u32[]{:S(2)}, u32[]{:S(2)}) async-start(bf16[2,64,1024]{2,0,1:T(2,128)(2,1)} %copy.77), calls=%async_computation.1 | async-start | bytes 524288 | tf_op jit(solution)/shard_map/all_to_all | solution.py:116
  72.8 1.2 copy.82
  74.7 7.6 %all-to-all-done.1 = bf16[2,64,1024]{2,0,1:T(2,128)(2,1)} async-done(((bf16[2,64,1024]{2,0,1:T(2,128)(2,1)}), bf16[2,64,1024]{2,0,1:T(2,128)(2,1)}, u32[]{:S(2)}, u32[]{:S(2)}) %all-to-all-start.1) | async-done | bytes 262176 | tf_op jit(solution)/shard_map/all_to_all | solution.py:116
  82.3 2.0 broadcast_in_dim.16
  84.4 7.7 %all-to-all-start.4 = ((bf16[4,64,2,1024]{3,1,2,0:T(8,128)(2,1)}), bf16[4,64,2,1024]{3,1,2,0:T(8,128)(2,1)}, u32[]{:S(2)}, u32[]{:S(2)}) async-start(bf16[4,64,2,1024]{3,1,2,0:T(8,128)(2,1)} %broadcast_in_dim.16), calls=%async_computation.4 | async-start | bytes 2097152 | tf_op jit(solution)/shard_map/all_to_all | solution.py:16
  92.0 1.2 copy.78
  93.9 11.7 %all-to-all-done.4 = bf16[4,64,2,1024]{3,1,2,0:T(8,128)(2,1)} async-done(((bf16[4,64,2,1024]{3,1,2,0:T(8,128)(2,1)}), bf16[4,64,2,1024]{3,1,2,0:T(8,128)(2,1)}, u32[]{:S(2)}, u32[]{:S(2)}) %all-to-all-start.4) | async-done | bytes 1048608 | tf_op jit(solution)/shard_map/all_to_all | solution.py:16
  105.6 2.0 broadcast_in_dim.14
  107.6 5.2 %all-to-all-start.2 = ((bf16[4,64,2,1024]{3,1,2,0:T(8,128)(2,1)}), bf16[4,64,2,1024]{3,1,2,0:T(8,128)(2,1)}, u32[]{:S(2)}, u32[]{:S(2)}) async-start(bf16[4,64,2,1024]{3,1,2,0:T(8,128)(2,1)} %broadcast_in_dim.14), calls=%async_computation.2 | async-start | bytes 2097152 | tf_op jit(solution)/shard_map/all_to_all | solution.py:16
  112.8 1.3 copy.84
  115.1 4.8 %fusion.45 = f32[2,256,1024]{2,1,0:T(8,128)} fusion(bf16[256,2,1024]{2,0,1:T(8,128)(2,1)S(1)} %bitcast.141, bf16[2,1024,1024]{2,1,0:T(8,128)(2,1)} %param.12), kind=kOutput, calls=%fused_computation.75 | convolution fusion | flops 1073741824 | bytes 7340032 | tf_op jit(solution)/shard_map/gjd,jdf->gjf/dot_general | solution.py:100
  119.9 6.5 %all-to-all-done.2 = bf16[4,64,2,1024]{3,1,2,0:T(8,128)(2,1)} async-done(((bf16[4,64,2,1024]{3,1,2,0:T(8,128)(2,1)}), bf16[4,64,2,1024]{3,1,2,0:T(8,128)(2,1)}, u32[]{:S(2)}, u32[]{:S(2)}) %all-to-all-start.2) | async-done | bytes 1048608 | tf_op jit(solution)/shard_map/all_to_all | solution.py:16
  126.4 1.5 copy.80
  128.3 4.7 %fusion.17 = bf16[256,2,1024]{2,0,1:T(8,128)(2,1)S(1)} fusion(f32[2,256,1024]{2,1,0:T(8,128)S(1)} %copy-done.5, bf16[256,2,1024]{2,0,1:T(8,128)(2,1)S(1)} %bitcast.153, bf16[2,1024,1024]{2,1,0:T(8,128)(2,1)} %param.13), kind=kOutput, calls=%fused_computation.23 | convolution fusion | flops 1084227584 | bytes 8388608 | tf_op jit(solution)/shard_map/gjd,jfd->gjf/dot_general | solution.py:121
  133.1 1.3 convolution_convert_fusion.5
  134.4 1.0 copy.85
  135.5 5.2 %all-to-all-start.5 = ((bf16[4,64,2,1024]{3,1,2,0:T(8,128)(2,1)}), bf16[4,64,2,1024]{3,1,2,0:T(8,128)(2,1)}, u32[]{:S(2)}, u32[]{:S(2)}) async-start(bf16[4,64,2,1024]{3,1,2,0:T(8,128)(2,1)} %copy.85), calls=%async_computation.5 | async-start | bytes 2097152 | tf_op jit(solution)/shard_map/all_to_all | solution.py:39
  140.6 4.2 %convolution_convert_fusion.4 = bf16[2,256,1024]{2,1,0:T(8,128)(2,1)S(1)} fusion(bf16[2,1024,1024]{2,1,0:T(8,128)(2,1)} %param.13, f32[2,256,1024]{2,1,0:T(8,128)} %fusion.45), kind=kOutput, calls=%fused_computation.37 | convolution fusion | flops 1078984704 | bytes 7340032 | tf_op jit(solution)/shard_map/gjf,jfd->gjd/dot_general | solution.py:104
  144.9 1.1 copy.89
  146.0 8.2 %all-to-all-done.5 = bf16[4,64,2,1024]{3,1,2,0:T(8,128)(2,1)} async-done(((bf16[4,64,2,1024]{3,1,2,0:T(8,128)(2,1)}), bf16[4,64,2,1024]{3,1,2,0:T(8,128)(2,1)}, u32[]{:S(2)}, u32[]{:S(2)}) %all-to-all-start.5) | async-done | bytes 1048608 | tf_op jit(solution)/shard_map/all_to_all | solution.py:39
  154.2 5.2 %all-to-all-start.7 = ((bf16[4,64,2,1024]{3,1,2,0:T(8,128)(2,1)}), bf16[4,64,2,1024]{3,1,2,0:T(8,128)(2,1)}, u32[]{:S(2)}, u32[]{:S(2)}) async-start(bf16[4,64,2,1024]{3,1,2,0:T(8,128)(2,1)} %copy.89), calls=%async_computation.7 | async-start | bytes 2097152 | tf_op jit(solution)/shard_map/all_to_all | solution.py:39
  159.4 2.2 reduce_sum.136
  161.6 1.9 copy.87
  163.5 9.5 %all-to-all-done.7 = bf16[4,64,2,1024]{3,1,2,0:T(8,128)(2,1)} async-done(((bf16[4,64,2,1024]{3,1,2,0:T(8,128)(2,1)}), bf16[4,64,2,1024]{3,1,2,0:T(8,128)(2,1)}, u32[]{:S(2)}, u32[]{:S(2)}) %all-to-all-start.7) | async-done | bytes 1048608 | tf_op jit(solution)/shard_map/all_to_all | solution.py:39
  173.0 4.6 %all-to-all-start.6 = ((bf16[64,2,1024]{2,1,0:T(2,128)(2,1)}), bf16[64,2,1024]{2,1,0:T(2,128)(2,1)}, u32[]{:S(2)}, u32[]{:S(2)}) async-start(bf16[64,2,1024]{2,1,0:T(2,128)(2,1)} %copy.87), calls=%async_computation.6 | async-start | bytes 524288 | tf_op jit(solution)/shard_map/all_to_all | solution.py:139
  177.6 2.2 reduce_sum.137
  179.8 1.9 copy.91
  181.7 5.5 %all-to-all-done.6 = bf16[64,2,1024]{2,1,0:T(2,128)(2,1)} async-done(((bf16[64,2,1024]{2,1,0:T(2,128)(2,1)}), bf16[64,2,1024]{2,1,0:T(2,128)(2,1)}, u32[]{:S(2)}, u32[]{:S(2)}) %all-to-all-start.6) | async-done | bytes 262176 | tf_op jit(solution)/shard_map/all_to_all | solution.py:139
  187.2 4.6 %all-to-all-start.8 = ((bf16[64,2,1024]{2,1,0:T(2,128)(2,1)}), bf16[64,2,1024]{2,1,0:T(2,128)(2,1)}, u32[]{:S(2)}, u32[]{:S(2)}) async-start(bf16[64,2,1024]{2,1,0:T(2,128)(2,1)} %copy.91), calls=%async_computation.8 | async-start | bytes 524288 | tf_op jit(solution)/shard_map/all_to_all | solution.py:110
  191.8 1.8 copy.88
  193.6 1.7 all_to_all.89
  195.4 5.9 %all-to-all-done.8 = bf16[64,2,1024]{2,1,0:T(2,128)(2,1)} async-done(((bf16[64,2,1024]{2,1,0:T(2,128)(2,1)}), bf16[64,2,1024]{2,1,0:T(2,128)(2,1)}, u32[]{:S(2)}, u32[]{:S(2)}) %all-to-all-start.8) | async-done | bytes 262176 | tf_op jit(solution)/shard_map/all_to_all | solution.py:110
  201.3 1.8 copy.92
  203.1 1.7 all_to_all.94
  204.9 1.8 convolution_bitcast_fusion
  207.4 1.9 fusion.37
  209.2 1.9 fusion.30
  211.1 2.4 fusion.5
  214.2 1.3 convolution_convert_fusion.2
  215.7 9.3 %all_to_all.112 = bf16[2,2,256,1024]{3,2,1,0:T(8,128)(2,1)} all-to-all(bf16[2,2,256,1024]{3,2,1,0:T(8,128)(2,1)S(1)} %bitcast.143), channel_id=1, replica_groups=mesh['img_0'=2,'img_1'=2,'exp'=32] {'img_1'}, dimensions={0} | all-to-all | bytes 4194304 | tf_op jit(solution)/shard_map/all_to_all | solution.py:39
  225.0 3.4 reduce_sum.141
  228.4 4.4 %all-to-all-start.10 = ((bf16[2,256,1024]{2,1,0:T(8,128)(2,1)}), bf16[2,256,1024]{2,1,0:T(8,128)(2,1)}, u32[]{:S(2)}, u32[]{:S(2)}) async-start(bf16[2,256,1024]{2,1,0:T(8,128)(2,1)} %reduce_sum.141), calls=%async_computation.10 | async-start | bytes 2097152 | tf_op jit(solution)/shard_map/all_to_all | solution.py:47
  232.8 5.1 %convolution_convert_fusion = bf16[2,1024,1024]{2,1,0:T(8,128)(2,1)} fusion(bf16[256,2,1024]{2,0,1:T(8,128)(2,1)S(1)} %bitcast.154, f32[2,256,1024]{2,1,0:T(8,128)} %fusion.45), kind=kOutput, calls=%fused_computation.4 | convolution fusion | flops 1080557568 | bytes 7340032 | tf_op jit(solution)/shard_map/gjf,gjd->jfd/dot_general | solution.py:125
  238.0 8.2 %all-to-all-done.10 = bf16[2,256,1024]{2,1,0:T(8,128)(2,1)} async-done(((bf16[2,256,1024]{2,1,0:T(8,128)(2,1)}), bf16[2,256,1024]{2,1,0:T(8,128)(2,1)}, u32[]{:S(2)}, u32[]{:S(2)}) %all-to-all-start.10) | async-done | bytes 1048608 | tf_op jit(solution)/shard_map/all_to_all | solution.py:47
  246.2 2.4 reduce_sum.142
  248.6 4.6 %all-to-all-start.11 = ((bf16[32,8,1024]{2,1,0:T(8,128)(2,1)}), bf16[32,8,1024]{2,1,0:T(8,128)(2,1)}, u32[]{:S(2)}, u32[]{:S(2)}) async-start(bf16[32,8,1024]{2,1,0:T(8,128)(2,1)} %bitcast.147), calls=%async_computation.11 | async-start | bytes 1048576 | tf_op jit(solution)/shard_map/all_to_all | solution.py:39
  253.3 4.5 %convolution_convert_fusion.1 = bf16[2,1024,1024]{2,1,0:T(8,128)(2,1)} fusion(bf16[256,2,1024]{2,0,1:T(8,128)(2,1)S(1)} %bitcast.142, bf16[256,2,1024]{2,0,1:T(8,128)(2,1)} %copy-done.11), kind=kOutput, calls=%fused_computation.5 | convolution fusion | flops 1075838976 | bytes 6291456 | tf_op jit(solution)/shard_map/gjd,gjf->jdf/dot_general | solution.py:128
  257.8 1.0 convolution_multiply_fusion
  258.8 6.4 %all-to-all-done.11 = bf16[32,8,1024]{2,1,0:T(8,128)(2,1)} async-done(((bf16[32,8,1024]{2,1,0:T(8,128)(2,1)}), bf16[32,8,1024]{2,1,0:T(8,128)(2,1)}, u32[]{:S(2)}, u32[]{:S(2)}) %all-to-all-start.11) | async-done | bytes 524320 | tf_op jit(solution)/shard_map/all_to_all | solution.py:39
  265.3 1.1 reduce_sum.143
  267.3 4.4 %all-to-all-start.12 = ((bf16[32,8,1024]{2,1,0:T(8,128)(2,1)}), bf16[32,8,1024]{2,1,0:T(8,128)(2,1)S(1)}, u32[]{:S(2)}, u32[]{:S(2)}) async-start(bf16[32,8,1024]{2,1,0:T(8,128)(2,1)} %broadcast_in_dim.17), calls=%async_computation.12 | async-start | bytes 1048576 | tf_op jit(solution)/shard_map/all_to_all | solution.py:16
  271.7 3.9 convolution_convert_fusion.3
  275.5 130.9 %all-reduce.2.cloned.1.call-done = f32[1024,64]{0,1:T(8,128)} async-done(((f32[1024,64]{0,1:T(8,128)}), f32[1024,64]{0,1:T(8,128)}) %all-reduce.2.cloned.1.call-update) | async-done | bytes 262160 | tf_op jit(solution)/shard_map/psum | solution.py:159
  406.4 1.2 multiply_reduce_fusion
  407.5 1.8 subtract_divide_fusion
  409.3 1.1 bitcast_convert_fusion
  (50 shorter events, 10.2 us)
Async XLA Ops:
  7.2 32.5 %copy-start = (bf16[2,256,1024]{2,1,0:T(8,128)(2,1)S(1)}, bf16[2,256,1024]{2,1,0:T(8,128)(2,1)}, u32[]{:S(2)}) copy-start(bf16[2,256,1024]{2,1,0:T(8,128)(2,1)} %param.7) | copy-start | bytes 3145732
  9.9 5.1 %copy-start.6 = (bf16[1024,64]{0,1:T(8,128)(2,1)S(1)}, bf16[1024,64]{0,1:T(8,128)(2,1)}, u32[]{:S(2)}) copy-start(bf16[1024,64]{0,1:T(8,128)(2,1)} %param.11) | copy-start | bytes 393220
  9.9 29.8 %all-to-all-start = ((bf16[4,256,1024]{2,1,0:T(8,128)(2,1)}), bf16[4,256,1024]{2,1,0:T(8,128)(2,1)S(1)}, u32[]{:S(2)}, u32[]{:S(2)}) async-start(bf16[4,256,1024]{2,1,0:T(8,128)(2,1)} %broadcast_in_dim.12), calls=%async_computation | async-start | bytes 4194304 | tf_op jit(solution)/shard_map/all_to_all | solution.py:16
  39.7 1.3 copy-start.7
  48.0 20.2 %all-to-all-start.3 = ((bf16[2,64,1024]{2,0,1:T(2,128)(2,1)}), bf16[2,64,1024]{2,0,1:T(2,128)(2,1)}, u32[]{:S(2)}, u32[]{:S(2)}) async-start(bf16[2,64,1024]{2,0,1:T(2,128)(2,1)} %copy.81), calls=%async_computation.3 | async-start | bytes 524288 | tf_op jit(solution)/shard_map/all_to_all | solution.py:98
  68.2 14.1 %all-to-all-start.1 = ((bf16[2,64,1024]{2,0,1:T(2,128)(2,1)}), bf16[2,64,1024]{2,0,1:T(2,128)(2,1)}, u32[]{:S(2)}, u32[]{:S(2)}) async-start(bf16[2,64,1024]{2,0,1:T(2,128)(2,1)} %copy.77), calls=%async_computation.1 | async-start | bytes 524288 | tf_op jit(solution)/shard_map/all_to_all | solution.py:116
  84.4 21.2 %all-to-all-start.4 = ((bf16[4,64,2,1024]{3,1,2,0:T(8,128)(2,1)}), bf16[4,64,2,1024]{3,1,2,0:T(8,128)(2,1)}, u32[]{:S(2)}, u32[]{:S(2)}) async-start(bf16[4,64,2,1024]{3,1,2,0:T(8,128)(2,1)} %broadcast_in_dim.16), calls=%async_computation.4 | async-start | bytes 2097152 | tf_op jit(solution)/shard_map/all_to_all | solution.py:16
  107.6 18.8 %all-to-all-start.2 = ((bf16[4,64,2,1024]{3,1,2,0:T(8,128)(2,1)}), bf16[4,64,2,1024]{3,1,2,0:T(8,128)(2,1)}, u32[]{:S(2)}, u32[]{:S(2)}) async-start(bf16[4,64,2,1024]{3,1,2,0:T(8,128)(2,1)} %broadcast_in_dim.14), calls=%async_computation.2 | async-start | bytes 2097152 | tf_op jit(solution)/shard_map/all_to_all | solution.py:16
  114.1 1.0 copy-start.1
  126.4 1.9 copy-start.5
  127.9 5.2 %copy-start.9 = (bf16[4,64,2,1024]{3,1,0,2:T(8,128)(2,1)}, bf16[4,64,2,1024]{3,1,0,2:T(8,128)(2,1)S(1)}, u32[]{:S(2)}) copy-start(bf16[4,64,2,1024]{3,1,0,2:T(8,128)(2,1)S(1)} %copy.80) | copy-start | bytes 3145732
  128.3 4.8 %copy-start.4 = (bf16[2,1024,1024]{2,1,0:T(8,128)(2,1)S(1)}, bf16[2,1024,1024]{2,1,0:T(8,128)(2,1)}, u32[]{:S(2)}) copy-start(bf16[2,1024,1024]{2,1,0:T(8,128)(2,1)} %param.12) | copy-start | bytes 12582916
  133.1 1.3 copy-start.11
  135.5 18.7 %all-to-all-start.5 = ((bf16[4,64,2,1024]{3,1,2,0:T(8,128)(2,1)}), bf16[4,64,2,1024]{3,1,2,0:T(8,128)(2,1)}, u32[]{:S(2)}, u32[]{:S(2)}) async-start(bf16[4,64,2,1024]{3,1,2,0:T(8,128)(2,1)} %copy.85), calls=%async_computation.5 | async-start | bytes 2097152 | tf_op jit(solution)/shard_map/all_to_all | solution.py:39
  154.2 18.8 %all-to-all-start.7 = ((bf16[4,64,2,1024]{3,1,2,0:T(8,128)(2,1)}), bf16[4,64,2,1024]{3,1,2,0:T(8,128)(2,1)}, u32[]{:S(2)}, u32[]{:S(2)}) async-start(bf16[4,64,2,1024]{3,1,2,0:T(8,128)(2,1)} %copy.89), calls=%async_computation.7 | async-start | bytes 2097152 | tf_op jit(solution)/shard_map/all_to_all | solution.py:39
  173.0 14.2 %all-to-all-start.6 = ((bf16[64,2,1024]{2,1,0:T(2,128)(2,1)}), bf16[64,2,1024]{2,1,0:T(2,128)(2,1)}, u32[]{:S(2)}, u32[]{:S(2)}) async-start(bf16[64,2,1024]{2,1,0:T(2,128)(2,1)} %copy.87), calls=%async_computation.6 | async-start | bytes 524288 | tf_op jit(solution)/shard_map/all_to_all | solution.py:139
  187.2 14.1 %all-to-all-start.8 = ((bf16[64,2,1024]{2,1,0:T(2,128)(2,1)}), bf16[64,2,1024]{2,1,0:T(2,128)(2,1)}, u32[]{:S(2)}, u32[]{:S(2)}) async-start(bf16[64,2,1024]{2,1,0:T(2,128)(2,1)} %copy.91), calls=%async_computation.8 | async-start | bytes 524288 | tf_op jit(solution)/shard_map/all_to_all | solution.py:110
  204.9 2.5 copy-start.8
  211.1 2.4 copy-start.3
  214.2 1.3 copy-start.12
  225.0 7.8 %copy-start.10 = (bf16[4,64,2,1024]{3,1,0,2:T(8,128)(2,1)S(1)}, bf16[4,64,2,1024]{3,1,0,2:T(8,128)(2,1)}, u32[]{:S(2)}) copy-start(bf16[4,64,2,1024]{3,1,0,2:T(8,128)(2,1)} %copy-done.9) | copy-start | bytes 3145732
  228.4 17.8 %all-to-all-start.10 = ((bf16[2,256,1024]{2,1,0:T(8,128)(2,1)}), bf16[2,256,1024]{2,1,0:T(8,128)(2,1)}, u32[]{:S(2)}, u32[]{:S(2)}) async-start(bf16[2,256,1024]{2,1,0:T(8,128)(2,1)} %reduce_sum.141), calls=%async_computation.10 | async-start | bytes 2097152 | tf_op jit(solution)/shard_map/all_to_all | solution.py:47
  238.0 15.3 %copy-start.2 = (bf16[4,64,2,1024]{3,1,0,2:T(8,128)(2,1)S(1)}, bf16[4,64,2,1024]{3,1,0,2:T(8,128)(2,1)}, u32[]{:S(2)}) copy-start(bf16[4,64,2,1024]{3,1,0,2:T(8,128)(2,1)} %copy-done.1) | copy-start | bytes 3145732
  248.6 16.7 %all-to-all-start.11 = ((bf16[32,8,1024]{2,1,0:T(8,128)(2,1)}), bf16[32,8,1024]{2,1,0:T(8,128)(2,1)}, u32[]{:S(2)}, u32[]{:S(2)}) async-start(bf16[32,8,1024]{2,1,0:T(8,128)(2,1)} %bitcast.147), calls=%async_computation.11 | async-start | bytes 1048576 | tf_op jit(solution)/shard_map/all_to_all | solution.py:39
  253.2 153.1 %all-reduce.2.cloned.1.call-start = ((), (), s32[]{:S(2)}) async-start(), calls=%async_computation.13 | async-start | bytes 524288 | tf_op jit(solution)/shard_map/psum | solution.py:159
  257.8 13.8 %copy-start.13 = (bf16[512,1024]{1,0:T(8,128)(2,1)S(1)}, bf16[512,1024]{1,0:T(8,128)(2,1)}, u32[]{:S(2)}) copy-start(bf16[512,1024]{1,0:T(8,128)(2,1)} %copy-done.12) | copy-start | bytes 3145732
  267.3 142.0 %all-to-all-start.12 = ((bf16[32,8,1024]{2,1,0:T(8,128)(2,1)}), bf16[32,8,1024]{2,1,0:T(8,128)(2,1)S(1)}, u32[]{:S(2)}, u32[]{:S(2)}) async-start(bf16[32,8,1024]{2,1,0:T(8,128)(2,1)} %broadcast_in_dim.17), calls=%async_computation.12 | async-start | bytes 1048576 | tf_op jit(solution)/shard_map/all_to_all | solution.py:16
Sparse Core Ops, SparseCore 0:
  259.3 146.9 all-reduce.1
where the time goes:
time: 419 us; the launch traced here: 417 us
  waiting for transfers between devices  232 us (55%)
  starting transfers between devices  66.1 us (16%)
  matrix products  44.4 us (11%)
  local copies, waits for them, and re-layouts  33.2 us (8%)
  other arithmetic  17.8 us (4%)
  between operations  14.3 us (3%)
  blocking collectives  9.33 us (2%)
    psum x1, waiting for transfers between devices, shards(): grad_unit = lax.psum(local_unit, IMG_EXP)  131 us
    all_to_all x4, waiting for transfers between devices, copy_for_each(): lax.all_to_all(jnp.broadcast_to(shard[None], (devices, *shard.shape)), ax...  42.7 us
    all_to_all x3, waiting for transfers between devices, summed_on_arrival(): lax.all_to_all(split_up(shard, dim, devices), axis, 0, 0, tiled=True)  24.1 us
    all_to_all x4, starting transfers between devices, copy_for_each(): lax.all_to_all(jnp.broadcast_to(shard[None], (devices, *shard.shape)), ax...  22.3 us
    all_to_all x3, starting transfers between devices, summed_on_arrival(): lax.all_to_all(split_up(shard, dim, devices), axis, 0, 0, tiled=True)  15 us
    all_to_all x1, starting transfers between devices, shards(): lax.all_to_all(slot_in, 'exp', split_axis=1, concat_axis=0, tiled=True)  10.6 us
    all_to_all x1, blocking collectives, summed_on_arrival(): lax.all_to_all(split_up(shard, dim, devices), axis, 0, 0, tiled=True)  9.33 us
    broadcast_in_dim x6, local copies, waits for them, and re-layouts, copy_for_each(): jnp.broadcast_to(shard[None], (devices, *shard.shape))  9.18 us
  transfers between devices with their start and end apart: 13, of which 12 were waited for; matrix products, arithmetic and copies ran while one was open for 11% of the time, Pallas kernels for 0%

commit v1 on v0

--- a/solution.py
+++ b/solution.py
@@ -156,7 +156,7 @@
         grad_logits, unit.T, preferred_element_type=jnp.float32
     )
     local_unit = factor * jnp.dot(normed.T, grad_logits, preferred_element_type=jnp.float32)
-    grad_unit = lax.psum(local_unit, IMG_EXP)
+    grad_unit = lax.psum(lax.psum(local_unit, "img_0"), ("img_1", "exp"))
     grad_slots = (
         grad_unit - unit32 * jnp.sum(unit32 * grad_unit, axis=0, keepdims=True)
     ) / slot_norm

time: 419 us -> 923 us (2.20)
  waiting for transfers between devices: 232 us -> 726 us
    psum x1 -> x2, waiting for transfers between devices: 131 us -> 631 us  [shards(): grad_unit = lax.psum(lax.psum(local_unit, 'img_0'), ('img_1', 'exp'))]
  transfers between devices with their start and end apart: 13 -> 14, of which waited for: 12 -> 12; matrix products, arithmetic and copies ran while one was open for 11% -> 5% of each run, Pallas kernels for 0% -> 0%
where the time goes in v1:
time: 923 us; the launch traced here: 916 us
  waiting for transfers between devices  726 us (79%)
  starting transfers between devices  70.9 us (8%)
  matrix products  44.4 us (5%)
  local copies, waits for them, and re-layouts  33.2 us (4%)
  other arithmetic  17.8 us (2%)
  between operations  14.4 us (2%)
  blocking collectives  9.33 us (1%)
    psum x2, waiting for transfers between devices, shards(): grad_unit = lax.psum(lax.psum(local_unit, 'img_0'), ('img_1', 'exp'))  631 us
    all_to_all x4, waiting for transfers between devices, copy_for_each(): lax.all_to_all(jnp.broadcast_to(shard[None], (devices, *shard.shape)), ax...  42.7 us
    all_to_all x4, starting transfers between devices, copy_for_each(): lax.all_to_all(jnp.broadcast_to(shard[None], (devices, *shard.shape)), ax...  27 us
  transfers between devices with their start and end apart: 14, of which 12 were waited for; matrix products, arithmetic and copies ran while one was open for 5% of the time, Pallas kernels for 0%

profile of v1, /device:TPU:1, one launch (start us, length us, event | category | flops | bytes accessed | tf_op | source)
XLA Modules:
  0.0 916.1 jit_solution(12971053558434021588)
XLA Ops:
  7.2 2.7 broadcast_in_dim.12
  9.9 5.1 all-to-all-start
  15.1 24.5 %all-to-all-done = bf16[4,256,1024]{2,1,0:T(8,128)(2,1)S(1)} async-done(((bf16[4,256,1024]{2,1,0:T(8,128)(2,1)}), bf16[4,256,1024]{2,1,0:T(8,128)(2,1)S(1)}, u32[]{:S(2)}, u32[]{:S(2)}) %all-to-all-start) | async-done | bytes 2097184 | tf_op jit(solution)/shard_map/all_to_all | solution.py:16
  39.7 1.3 copy-done.7
  41.0 3.2 fusion.10
  48.0 10.6 %all-to-all-start.3 = ((bf16[2,64,1024]{2,0,1:T(2,128)(2,1)}), bf16[2,64,1024]{2,0,1:T(2,128)(2,1)}, u32[]{:S(2)}, u32[]{:S(2)}) async-start(bf16[2,64,1024]{2,0,1:T(2,128)(2,1)} %copy.81), calls=%async_computation.3 | async-start | bytes 524288 | tf_op jit(solution)/shard_map/all_to_all | solution.py:98
  58.7 1.5 convolution_convert_fusion.7
  61.2 7.1 all-to-all-done.3
  68.2 4.6 all-to-all-start.1
  72.8 1.2 copy.82
  74.7 7.6 all-to-all-done.1
  82.3 2.0 broadcast_in_dim.16
  84.4 7.7 all-to-all-start.4
  92.0 1.2 copy.78
  93.9 11.7 %all-to-all-done.4 = bf16[4,64,2,1024]{3,1,2,0:T(8,128)(2,1)} async-done(((bf16[4,64,2,1024]{3,1,2,0:T(8,128)(2,1)}), bf16[4,64,2,1024]{3,1,2,0:T(8,128)(2,1)}, u32[]{:S(2)}, u32[]{:S(2)}) %all-to-all-start.4) | async-done | bytes 1048608 | tf_op jit(solution)/shard_map/all_to_all | solution.py:16
  105.6 2.0 broadcast_in_dim.14
  107.6 5.2 all-to-all-start.2
  112.8 1.3 copy.84
  115.1 4.8 fusion.45
  119.9 6.5 all-to-all-done.2
  126.4 1.5 copy.80
  128.3 4.7 fusion.17
  133.1 1.3 convolution_convert_fusion.5
  134.4 1.0 copy.85
  135.5 5.2 all-to-all-start.5
  140.6 4.2 convolution_convert_fusion.4
  144.9 1.1 copy.89
  146.0 8.2 all-to-all-done.5
  154.2 5.2 all-to-all-start.7
  159.4 2.2 reduce_sum.136
  161.6 1.9 copy.87
  163.5 9.5 %all-to-all-done.7 = bf16[4,64,2,1024]{3,1,2,0:T(8,128)(2,1)} async-done(((bf16[4,64,2,1024]{3,1,2,0:T(8,128)(2,1)}), bf16[4,64,2,1024]{3,1,2,0:T(8,128)(2,1)}, u32[]{:S(2)}, u32[]{:S(2)}) %all-to-all-start.7) | async-done | bytes 1048608 | tf_op jit(solution)/shard_map/all_to_all | solution.py:39
  173.0 4.6 all-to-all-start.6
  177.6 2.2 reduce_sum.137
  179.8 1.9 copy.91
  181.7 5.5 all-to-all-done.6
  187.2 4.6 all-to-all-start.8
  191.8 1.8 copy.88
  193.6 1.7 all_to_all.89
  195.4 5.9 all-to-all-done.8
  201.3 1.8 copy.92
  203.1 1.7 all_to_all.94
  204.9 1.8 convolution_bitcast_fusion
  207.4 1.9 fusion.37
  209.2 1.9 fusion.30
  211.1 2.4 fusion.5
  214.2 1.3 convolution_convert_fusion.2
  215.7 9.3 %all_to_all.112 = bf16[2,2,256,1024]{3,2,1,0:T(8,128)(2,1)} all-to-all(bf16[2,2,256,1024]{3,2,1,0:T(8,128)(2,1)S(1)} %bitcast.143), channel_id=1, replica_groups=mesh['img_0'=2,'img_1'=2,'exp'=32] {'img_1'}, dimensions={0} | all-to-all | bytes 4194304 | tf_op jit(solution)/shard_map/all_to_all | solution.py:39
  225.0 3.4 reduce_sum.141
  228.4 4.4 all-to-all-start.10
  232.8 5.1 convolution_convert_fusion
  238.0 8.2 all-to-all-done.10
  246.2 2.4 reduce_sum.142
  248.6 4.6 all-to-all-start.11
  253.3 1.0 convolution_multiply_fusion
  254.4 4.5 convolution_convert_fusion.1
  258.9 29.5 %all-reduce.3.cloned.1.call-done = f32[1024,64]{0,1:T(8,128)} async-done(((f32[1024,64]{0,1:T(8,128)}), f32[1024,64]{0,1:T(8,128)}) %all-reduce.3.cloned.1.call-update) | async-done | bytes 262160 | tf_op jit(solution)/shard_map/psum | solution.py:159
  288.5 1.1 reduce_sum.143
  290.5 9.1 all-to-all-start.12
  299.6 3.8 convolution_convert_fusion.3
  303.4 601.8 %all-reduce.5.cloned.1.call-done = f32[1024,64]{0,1:T(8,128)} async-done(((f32[1024,64]{0,1:T(8,128)}), f32[1024,64]{0,1:T(8,128)}) %all-reduce.5.cloned.1.call-update) | async-done | bytes 262160 | tf_op jit(solution)/shard_map/psum | solution.py:159
  905.3 1.2 multiply_reduce_fusion
  906.4 1.8 subtract_divide_fusion
  908.2 1.1 bitcast_convert_fusion
  (53 shorter events, 10.3 us)
Async XLA Ops:
  7.2 32.5 %copy-start = (bf16[2,256,1024]{2,1,0:T(8,128)(2,1)S(1)}, bf16[2,256,1024]{2,1,0:T(8,128)(2,1)}, u32[]{:S(2)}) copy-start(bf16[2,256,1024]{2,1,0:T(8,128)(2,1)} %param.7) | copy-start | bytes 3145732
  9.9 5.1 copy-start.6
  9.9 29.8 %all-to-all-start = ((bf16[4,256,1024]{2,1,0:T(8,128)(2,1)}), bf16[4,256,1024]{2,1,0:T(8,128)(2,1)S(1)}, u32[]{:S(2)}, u32[]{:S(2)}) async-start(bf16[4,256,1024]{2,1,0:T(8,128)(2,1)} %broadcast_in_dim.12), calls=%async_computation | async-start | bytes 4194304 | tf_op jit(solution)/shard_map/all_to_all | solution.py:16
  39.7 1.3 copy-start.7
  48.0 20.2 %all-to-all-start.3 = ((bf16[2,64,1024]{2,0,1:T(2,128)(2,1)}), bf16[2,64,1024]{2,0,1:T(2,128)(2,1)}, u32[]{:S(2)}, u32[]{:S(2)}) async-start(bf16[2,64,1024]{2,0,1:T(2,128)(2,1)} %copy.81), calls=%async_computation.3 | async-start | bytes 524288 | tf_op jit(solution)/shard_map/all_to_all | solution.py:98
  68.2 14.1 %all-to-all-start.1 = ((bf16[2,64,1024]{2,0,1:T(2,128)(2,1)}), bf16[2,64,1024]{2,0,1:T(2,128)(2,1)}, u32[]{:S(2)}, u32[]{:S(2)}) async-start(bf16[2,64,1024]{2,0,1:T(2,128)(2,1)} %copy.77), calls=%async_computation.1 | async-start | bytes 524288 | tf_op jit(solution)/shard_map/all_to_all | solution.py:116
  84.4 21.2 %all-to-all-start.4 = ((bf16[4,64,2,1024]{3,1,2,0:T(8,128)(2,1)}), bf16[4,64,2,1024]{3,1,2,0:T(8,128)(2,1)}, u32[]{:S(2)}, u32[]{:S(2)}) async-start(bf16[4,64,2,1024]{3,1,2,0:T(8,128)(2,1)} %broadcast_in_dim.16), calls=%async_computation.4 | async-start | bytes 2097152 | tf_op jit(solution)/shard_map/all_to_all | solution.py:16
  107.6 18.8 %all-to-all-start.2 = ((bf16[4,64,2,1024]{3,1,2,0:T(8,128)(2,1)}), bf16[4,64,2,1024]{3,1,2,0:T(8,128)(2,1)}, u32[]{:S(2)}, u32[]{:S(2)}) async-start(bf16[4,64,2,1024]{3,1,2,0:T(8,128)(2,1)} %broadcast_in_dim.14), calls=%async_computation.2 | async-start | bytes 2097152 | tf_op jit(solution)/shard_map/all_to_all | solution.py:16
  114.1 1.0 copy-start.1
  126.4 1.9 copy-start.5
  127.9 5.2 copy-start.9
  128.3 4.8 copy-start.4
  133.1 1.3 copy-start.11
  135.5 18.7 %all-to-all-start.5 = ((bf16[4,64,2,1024]{3,1,2,0:T(8,128)(2,1)}), bf16[4,64,2,1024]{3,1,2,0:T(8,128)(2,1)}, u32[]{:S(2)}, u32[]{:S(2)}) async-start(bf16[4,64,2,1024]{3,1,2,0:T(8,128)(2,1)} %copy.85), calls=%async_computation.5 | async-start | bytes 2097152 | tf_op jit(solution)/shard_map/all_to_all | solution.py:39
  154.2 18.8 %all-to-all-start.7 = ((bf16[4,64,2,1024]{3,1,2,0:T(8,128)(2,1)}), bf16[4,64,2,1024]{3,1,2,0:T(8,128)(2,1)}, u32[]{:S(2)}, u32[]{:S(2)}) async-start(bf16[4,64,2,1024]{3,1,2,0:T(8,128)(2,1)} %copy.89), calls=%async_computation.7 | async-start | bytes 2097152 | tf_op jit(solution)/shard_map/all_to_all | solution.py:39
  173.0 14.2 %all-to-all-start.6 = ((bf16[64,2,1024]{2,1,0:T(2,128)(2,1)}), bf16[64,2,1024]{2,1,0:T(2,128)(2,1)}, u32[]{:S(2)}, u32[]{:S(2)}) async-start(bf16[64,2,1024]{2,1,0:T(2,128)(2,1)} %copy.87), calls=%async_computation.6 | async-start | bytes 524288 | tf_op jit(solution)/shard_map/all_to_all | solution.py:139
  187.2 14.1 %all-to-all-start.8 = ((bf16[64,2,1024]{2,1,0:T(2,128)(2,1)}), bf16[64,2,1024]{2,1,0:T(2,128)(2,1)}, u32[]{:S(2)}, u32[]{:S(2)}) async-start(bf16[64,2,1024]{2,1,0:T(2,128)(2,1)} %copy.91), calls=%async_computation.8 | async-start | bytes 524288 | tf_op jit(solution)/shard_map/all_to_all | solution.py:110
  204.9 2.5 copy-start.8
  211.1 2.4 copy-start.3
  214.2 1.3 copy-start.12
  225.0 7.8 copy-start.10
  228.4 17.8 %all-to-all-start.10 = ((bf16[2,256,1024]{2,1,0:T(8,128)(2,1)}), bf16[2,256,1024]{2,1,0:T(8,128)(2,1)}, u32[]{:S(2)}, u32[]{:S(2)}) async-start(bf16[2,256,1024]{2,1,0:T(8,128)(2,1)} %reduce_sum.141), calls=%async_computation.10 | async-start | bytes 2097152 | tf_op jit(solution)/shard_map/all_to_all | solution.py:47
  238.0 16.4 %copy-start.2 = (bf16[4,64,2,1024]{3,1,0,2:T(8,128)(2,1)S(1)}, bf16[4,64,2,1024]{3,1,0,2:T(8,128)(2,1)}, u32[]{:S(2)}) copy-start(bf16[4,64,2,1024]{3,1,0,2:T(8,128)(2,1)} %copy-done.1) | copy-start | bytes 3145732
  248.6 39.9 %all-to-all-start.11 = ((bf16[32,8,1024]{2,1,0:T(8,128)(2,1)}), bf16[32,8,1024]{2,1,0:T(8,128)(2,1)}, u32[]{:S(2)}, u32[]{:S(2)}) async-start(bf16[32,8,1024]{2,1,0:T(8,128)(2,1)} %bitcast.147), calls=%async_computation.11 | async-start | bytes 1048576 | tf_op jit(solution)/shard_map/all_to_all | solution.py:39
  253.2 35.2 %all-reduce.3.cloned.1.call-start = ((), (), s32[]{:S(2)}) async-start(), calls=%async_computation.13 | async-start | bytes 524288 | tf_op jit(solution)/shard_map/psum | solution.py:159
  254.3 651.0 %all-reduce.5.cloned.1.call-start = ((), (), s32[]{:S(2)}) async-start(), calls=%async_computation.14 | async-start | bytes 524288 | tf_op jit(solution)/shard_map/psum | solution.py:159
  258.9 40.7 %copy-start.13 = (bf16[512,1024]{1,0:T(8,128)(2,1)S(1)}, bf16[512,1024]{1,0:T(8,128)(2,1)}, u32[]{:S(2)}) copy-start(bf16[512,1024]{1,0:T(8,128)(2,1)} %copy-done.12) | copy-start | bytes 3145732
  290.5 617.7 %all-to-all-start.12 = ((bf16[32,8,1024]{2,1,0:T(8,128)(2,1)}), bf16[32,8,1024]{2,1,0:T(8,128)(2,1)S(1)}, u32[]{:S(2)}, u32[]{:S(2)}) async-start(bf16[32,8,1024]{2,1,0:T(8,128)(2,1)} %broadcast_in_dim.17), calls=%async_computation.12 | async-start | bytes 1048576 | tf_op jit(solution)/shard_map/all_to_all | solution.py:16
Sparse Core Ops, SparseCore 0:
  257.0 31.3 all-reduce.2
  290.9 614.2 all-reduce.4
